TPU v7x, 32 devices: a whole 2x2x4 slice. The times are simulated.
32 devices in a mesh: group: 2 (over y), chan: 4 (over z), tm: 2 (over x), beam: 2 (over core).
Axes of the slice: x: 2, y: 2, z: 4, core: 2. Of those that a mesh axis runs over, the one named last changes fastest.
Arguments:
- samples: bfloat16 [1024, 2, 1024, 16], P(('group', 'chan', 'beam'), None, None, 'tm'), parts along dimension 0, may hold values from -6 to 6
- window_taps: float32 [4, 1024], replicated, may hold values from -1 to 1
- sky_model: bfloat16 [1024, 2, 512, 512], P(('group', 'chan', 'tm'), None, 'beam'), parts along dimension 0, may hold values from -0.0234375 to 0.0234375
- prior_gains: float32 [1024, 2, 512], P(('group', 'chan', 'tm')), parts along dimension 0, may hold values from -4.2 to 4.2
- beam_steering: int32 [2, 1024], P(None, ('group', 'beam')), parts along dimension 1, may hold values from 0 to 255
- input_flags: int32 [1024, 512], P(('group', 'chan', 'tm')), parts along dimension 0, may hold values 0 or 1
Outputs:
- visibilities: bfloat16 [1024, 2, 512, 512], P(('group', 'chan', 'tm'), None, 'beam'), parts along dimension 0
- new_gains: float32 [1024, 2, 512], P(('group', 'chan', 'tm'), None, 'beam'), parts along dimension 0
- beam_power: float32 [1024, 512, 16], P(('group', 'chan', 'tm'), 'beam'), parts along dimension 0
There are 2 independent parts, one for each index of `group`. A program takes and returns all parts, laid end to end along the dimension named above; an argument that names none is the same for every part. Nothing has to cross between parts.
All inputs are finite; a program needn't handle non-finite values. No bound on the sum of `input_flags` on one device may be relied on, other than what follows from the above.
Results may differ from a plain program's by a relative error of at most 0.0076.
Values may be sent and summed in bfloat16 or wider, within the bound.
A program may use at most 384 MiB of HBM per device.

v0:
```python
import math

import jax
import jax.numpy as jnp
from jax import lax
from jax.sharding import PartitionSpec as P

NCH = 512
ITERS = 2


damping = 0.5
epsilon = 1e-06


def from_behind(block, axis, distance):
    devices = range(lax.axis_size(axis))
    route = [(i - distance, i) for i in devices if i - distance in devices]
    return lax.ppermute(block, axis, route)


def filter_bank(extended, window_taps, kept_count, frames):
    transform_count = window_taps.shape[1]
    tap_count = window_taps.shape[0]
    local_inputs = extended.shape[0]
    kept = jnp.arange(kept_count, dtype=jnp.int32)
    indices = jnp.arange(transform_count, dtype=jnp.int32)
    phases = (kept[:, None] * indices[None, :] % transform_count).astype(jnp.float32) * (
        2.0 * math.pi / transform_count
    )
    cosine = jnp.cos(phases)
    sine_part = jnp.sin(phases)
    real_in = extended[:, :transform_count]
    imag_in = extended[:, transform_count:]
    real_sum = jnp.zeros((local_inputs, kept_count, frames), jnp.float32)
    imag_sum = jnp.zeros((local_inputs, kept_count, frames), jnp.float32)
    for tap_index in range(tap_count):
        tap_row = window_taps[tap_index][None, :]
        cos_block = (cosine * tap_row / math.sqrt(transform_count)).astype(jnp.bfloat16)
        sin_block = (sine_part * tap_row / math.sqrt(transform_count)).astype(jnp.bfloat16)
        part_real = real_in[:, :, tap_index : tap_index + frames]
        part_imag = imag_in[:, :, tap_index : tap_index + frames]
        real_sum = (
            real_sum
            + jnp.einsum("kn,inf->ikf", cos_block, part_real, preferred_element_type=jnp.float32)
            + jnp.einsum("kn,inf->ikf", sin_block, part_imag, preferred_element_type=jnp.float32)
        )
        imag_sum = (
            imag_sum
            + jnp.einsum("kn,inf->ikf", cos_block, part_imag, preferred_element_type=jnp.float32)
            - jnp.einsum("kn,inf->ikf", sin_block, part_real, preferred_element_type=jnp.float32)
        )
    return jnp.stack([real_sum, imag_sum], axis=2).astype(jnp.bfloat16)


def steering_angles(beam_steering, channels, input_count, chan_total):
    positions = jnp.arange(input_count, dtype=jnp.int32)
    column = positions // (input_count // 4)
    within = positions % (input_count // 4)
    phase_index = (
        beam_steering[0][:, None] * column[None, :] * 64
        + beam_steering[1][:, None] * within[None, :]
    ) % 256
    scaled = phase_index[None] * (chan_total + channels)[:, None, None]
    return scaled.astype(jnp.float32) * (2.0 * math.pi / (512 * chan_total))


def cross_rows(owned_rows, all_rows):
    paired = owned_rows.reshape(owned_rows.shape[0], owned_rows.shape[1], -1)
    rotated = jnp.stack([owned_rows[:, :, 1], -owned_rows[:, :, 0]], axis=2).reshape(paired.shape)
    left = jnp.stack([paired, rotated], axis=1)
    columns = all_rows.reshape(all_rows.shape[0], all_rows.shape[1], -1)
    return jnp.einsum("isck,jck->csij", left, columns, preferred_element_type=jnp.float32)


def form_beams(whole_set, gains_part, weights, beam_steering, channels, chan_total):
    input_count = whole_set.shape[0]
    angles = steering_angles(beam_steering, channels, input_count, chan_total)
    cosine = jnp.cos(angles)
    sine_part = jnp.sin(angles)
    scale_factor = 1.0 / math.sqrt(input_count)
    gain_real = (gains_part[:, 0] * weights)[:, None, :]
    gain_imaginary = (gains_part[:, 1] * weights)[:, None, :]
    steering_real = ((gain_real * cosine - gain_imaginary * sine_part) * scale_factor).astype(
        jnp.bfloat16
    )
    steering_imaginary = ((gain_real * sine_part + gain_imaginary * cosine) * scale_factor).astype(
        jnp.bfloat16
    )
    spectrum_real = whole_set[:, :, 0]
    spectrum_imaginary = whole_set[:, :, 1]
    volt_real = jnp.einsum(
        "jan,njg->jag", steering_real, spectrum_real, preferred_element_type=jnp.float32
    ) - jnp.einsum(
        "jan,njg->jag", steering_imaginary, spectrum_imaginary, preferred_element_type=jnp.float32
    )
    volt_imag = jnp.einsum(
        "jan,njg->jag", steering_real, spectrum_imaginary, preferred_element_type=jnp.float32
    ) + jnp.einsum(
        "jan,njg->jag", steering_imaginary, spectrum_real, preferred_element_type=jnp.float32
    )
    return volt_real * volt_real + volt_imag * volt_imag


def matvec(matrix, vector):
    return jnp.einsum("crj,cj->cr", matrix, vector, precision=lax.Precision.HIGHEST)


def shards(samples, window_taps, sky_model, prior_gains, beam_steering, input_flags):
    local_inputs = samples.shape[0]
    transform_count = samples.shape[2]
    frames = samples.shape[3]
    tap_count = window_taps.shape[0]
    kept_count = NCH
    time_count = lax.axis_size("tm")
    beam_count = lax.axis_size("beam")
    time_index = lax.axis_index("tm")
    beam_index = lax.axis_index("beam")
    chan_index = lax.axis_index("chan")
    weights = input_flags.astype(jnp.float32)
    stacked = samples.reshape(local_inputs, 2 * transform_count, frames)
    previous = from_behind(stacked[:, :, frames - tap_count + 1 :], "tm", 1)
    extended = jnp.concatenate([previous, stacked], axis=2)
    spectra = filter_bank(extended, window_taps, kept_count, frames).reshape(
        1, local_inputs, kept_count, 2, 1, frames
    )
    mixed = lax.all_to_all(spectra, ("chan", "tm"), split_axis=2, concat_axis=0, tiled=True)
    blocks = mixed.reshape(
        mixed.shape[0] // time_count, time_count, local_inputs, mixed.shape[2], 2, frames
    )
    turned = jnp.transpose(blocks, (0, 2, 3, 4, 1, 5))
    joined = lax.all_gather(turned, "beam", axis=1, tiled=True)
    input_count = joined.shape[0] * joined.shape[1]
    chan_local = joined.shape[2]
    whole_set = joined.reshape(input_count, chan_local, 2, joined.shape[4] * frames)
    half_rows = input_count // beam_count
    owned_rows = lax.dynamic_slice_in_dim(whole_set, beam_index * half_rows, half_rows, 0)
    terms = cross_rows(owned_rows, whole_set)
    visibilities = (terms / whole_set.shape[3]).astype(jnp.bfloat16)
    channels = (chan_index * time_count + time_index) * chan_local + jnp.arange(
        chan_local, dtype=jnp.int32
    )
    beam_power = form_beams(whole_set, prior_gains, weights, beam_steering, channels, kept_count)
    vis_used = lax.optimization_barrier(visibilities).astype(jnp.float32)
    model_values = sky_model.astype(jnp.float32)
    weighted = jnp.stack(
        [
            vis_used[:, 0] * model_values[:, 0] + vis_used[:, 1] * model_values[:, 1],
            vis_used[:, 1] * model_values[:, 0] - vis_used[:, 0] * model_values[:, 1],
        ],
        axis=1,
    )
    model_power = model_values[:, 0] * model_values[:, 0] + model_values[:, 1] * model_values[:, 1]
    row_start = beam_index * half_rows
    current = prior_gains
    updated = lax.dynamic_slice_in_dim(current, row_start, half_rows, 2)
    for step_index in range(ITERS):
        masked_real = current[:, 0] * weights
        masked_imag = current[:, 1] * weights
        vectors = jnp.stack([masked_real, masked_imag], axis=2)
        products = jnp.einsum("csrj,cjv->csrv", weighted, vectors, precision=lax.Precision.HIGHEST)
        numer_real = products[:, 0, :, 0] - products[:, 1, :, 1]
        numer_imag = products[:, 0, :, 1] + products[:, 1, :, 0]
        denom = (
            matvec(
                model_power,
                weights * (current[:, 0] * current[:, 0] + current[:, 1] * current[:, 1]),
            )
            + epsilon
        )
        older = lax.dynamic_slice_in_dim(current, row_start, half_rows, 2)
        updated = damping * older + (1.0 - damping) * jnp.stack(
            [numer_real / denom, numer_imag / denom], axis=1
        )
        if step_index + 1 < ITERS:
            current = lax.all_gather(updated, "beam", axis=2, tiled=True)
    return (visibilities, updated, beam_power)


def solution(mesh):
    return jax.shard_map(
        shards,
        mesh=mesh,
        in_specs=(
            P(("group", "chan", "beam"), None, None, "tm"),
            P(),
            P(("group", "chan", "tm"), None, "beam", None),
            P(("group", "chan", "tm"), None, None),
            P(None, ("group", "beam")),
            P(("group", "chan", "tm"), None),
        ),
        out_specs=(
            P(("group", "chan", "tm"), None, "beam", None),
            P(("group", "chan", "tm"), None, "beam"),
            P(("group", "chan", "tm"), "beam", None),
        ),
        check_vma=False,
    )
```

profile of v0, /device:TPU:0, one launch (start us, length us, event | category | flops | bytes accessed | tf_op | source)
XLA Modules:
  0.0 1086.7 jit_solution(5787775991752032830)
XLA Ops:
  15.1 8.4 convolution_bitcast_fusion
  23.5 8.7 convolution_bitcast_fusion.1
  32.2 8.6 convolution_bitcast_fusion.2
  40.8 8.4 convolution_bitcast_fusion.3
  49.9 8.6 fusion.76
  58.5 8.8 fusion.74
  67.2 8.7 fusion.60
  75.9 8.4 fusion.62
  86.2 8.1 fusion.70
  94.3 8.6 fusion.68
  102.8 8.3 fusion.66
  111.2 8.1 fusion.72
  119.2 8.4 fusion.58
  127.6 8.5 fusion.64
  136.1 8.5 fusion.43
  144.6 8.7 fusion.44
  166.7 44.5 %copy.137 = bf16[64,2,256,512]{2,3,1,0:T(8,128)(2,1)} copy(bf16[64,2,256,512]{3,2,1,0:T(8,128)(2,1)} %param.8) | data formatting | bytes 67108864 | tf_op args[2]
  211.2 32.8 %convert_element_type.85 = f32[64,2,256,512]{2,3,1,0:T(8,128)} convert(bf16[64,2,256,512]{2,3,1,0:T(8,128)(2,1)} %copy.137) | non-fusion elementwise | flops 16777216 | bytes 100663296 | tf_op jit(solution)/shard_map/convert_element_type | solution.py:145
  256.9 29.3 %fusion.5 = f32[64,1,256]{2,1,0:T(1,128)} fusion(f32[64,2,256,512]{2,3,1,0:T(8,128)} %convert_element_type.85, f32[64,512,1]{1,0,2:T(8,128)S(1)} %copy-done.13), kind=kOutput, calls=%fused_computation.7 | convolution fusion | flops 125829120 | bytes 67305472 | tf_op jit(solution)/shard_map/crj,cj->cr/dot_general | solution.py:106
  286.2 7.8 copy.133
  294.1 127.1 %fusion.9 = f32[64,256,16]{1,2,0:T(8,128)} fusion(f32[64,512]{1,0:T(8,128)S(1)} %get-tuple-element.37, s32[64]{0:T(128)S(1)} %add_add_fusion, s32[256,512]{1,0:T(8,128)S(1)} %copy-done.5, f32[64,512]{1,0:T(8,128)S(1)} %copy-done.8, bf16[512,64,2,16]{0,3,1,2:T(8,128)(2,1)S(1)} %bitcast.221), kind=kOutput, calls=%fused_computation.17 | convolution fusion | flops 335544320 | bytes 2884096 | tf_op jit(solution)/shard_map/jan,njg->jag/dot_general | solution.py:97
  421.2 126.8 %fusion.10 = f32[64,256,16]{1,2,0:T(8,128)} fusion(f32[64,512]{1,0:T(8,128)S(1)} %get-tuple-element.37, s32[64]{0:T(128)S(1)} %add_add_fusion, s32[256,512]{1,0:T(8,128)S(1)} %copy-done.5, f32[64,512]{1,0:T(8,128)S(1)} %copy-done.8, bf16[512,64,2,16]{0,3,1,2:T(8,128)(2,1)S(1)} %bitcast.222), kind=kOutput, calls=%fused_computation.18 | convolution fusion | flops 335544320 | bytes 2884096 | tf_op jit(solution)/shard_map/jan,njg->jag/dot_general | solution.py:92
  549.6 7.8 copy.132
  557.4 15.4 %fusion.2 = bf16[64,2,256,512]{2,3,1,0:T(8,128)(2,1)} fusion(bf16[512,64,32,1]{0,2,3,1:T(8,128)(2,1)S(1)} %bitcast.220, bf16[256,1,64,32]{0,3,1,2:T(8,128)(2,1)S(1)} %bitcast.243, bf16[256,1,64,32]{0,3,1,2:T(8,128)(2,1)} %bitcast.244), kind=kOutput, calls=%fused_computation.4 | convolution fusion | flops 1111490560 | bytes 37748736 | tf_op jit(solution)/shard_map/isck,jck->csij/dot_general | solution.py:73
  572.8 44.6 %copy.152 = bf16[64,2,256,512]{3,2,1,0:T(8,128)(2,1)} copy(bf16[64,2,256,512]{2,3,1,0:T(8,128)(2,1)} %fusion.2) | data formatting | bytes 67108864
  617.4 127.7 %fusion.26 = f32[64,256,16]{1,2,0:T(8,128)} fusion(f32[64,256,16]{1,2,0:T(8,128)} %fusion.9, f32[64,512]{1,0:T(8,128)S(1)} %get-tuple-element.37, s32[64]{0:T(128)S(1)} %add_add_fusion, s32[256,512]{1,0:T(8,128)S(1)} %copy-done.6, f32[64,512]{1,0:T(8,128)S(1)} %copy-done.8, bf16[512,64,2,16]{0,3,1,2:T(8,128)(2,1)S(1)} %bitcast.225), kind=kOutput, calls=%fused_computation.55 | convolution fusion | flops 336068608 | bytes 3932672 | tf_op jit(solution)/shard_map/jan,njg->jag/dot_general | solution.py:99
  745.1 32.7 %convert_element_type.84 = f32[64,2,256,512]{2,3,1,0:T(8,128)} convert(bf16[64,2,256,512]{2,3,1,0:T(8,128)(2,1)} %fusion.2) | non-fusion elementwise | flops 16777216 | bytes 100663296 | tf_op jit(solution)/shard_map/convert_element_type | solution.py:144
  777.8 64.6 %multiply_add_fusion.1 = (f32[64,1,256,512]{2,3,1,0:T(8,128)}, f32[64,1,256,512]{2,3,1,0:T(8,128)}) fusion(f32[64,2,256,512]{2,3,1,0:T(8,128)} %convert_element_type.84, f32[64,2,256,512]{2,3,1,0:T(8,128)} %convert_element_type.85), kind=kLoop, calls=%fused_computation.16 | loop fusion | flops 50331648 | bytes 201326592 | tf_op jit(solution)/shard_map/add | solution.py:148
  842.4 39.1 %fusion.1 = f32[64,2,256,2]{2,3,1,0:T(2,128)S(1)} fusion(f32[64,1,256,512]{2,3,1,0:T(8,128)} %get-tuple-element.19, f32[64,1,256,512]{2,3,1,0:T(8,128)} %get-tuple-element.18, f32[64,512,1]{1,2,0:T(1,128)S(1)} %copy-done.12, f32[64,512,1]{1,2,0:T(1,128)S(1)} %copy-done.11), kind=kOutput, calls=%fused_computation.3 | convolution fusion | flops 419495936 | bytes 67633152 | tf_op jit(solution)/shard_map/csrj,cjv->csrv/dot_general | solution.py:161
  883.9 27.3 %fusion.3 = f32[64,1,256]{2,1,0:T(1,128)S(1)} fusion(f32[64,2,256,512]{2,3,1,0:T(8,128)} %convert_element_type.85, f32[64,512,1]{1,0,2:T(8,128)S(1)} %get-tuple-element.25), kind=kOutput, calls=%fused_computation.5 | convolution fusion | flops 125829120 | bytes 67305472 | tf_op jit(solution)/shard_map/crj,cj->cr/dot_general | solution.py:106
  911.2 39.3 %fusion = f32[64,2,256,2]{2,3,1,0:T(2,128)S(1)} fusion(f32[64,1,256,512]{2,3,1,0:T(8,128)} %get-tuple-element.19, f32[64,1,256,512]{2,3,1,0:T(8,128)} %get-tuple-element.18, f32[64,512,2,1]{1,0,2,3:T(8,128)S(1)} %maximum_bitcast_fusion.2), kind=kOutput, calls=%fused_computation.2 | convolution fusion | flops 419430400 | bytes 67633152 | tf_op jit(solution)/shard_map/csrj,cjv->csrv/dot_general | solution.py:161
  951.5 128.0 %fusion.24 = f32[64,256,16]{1,2,0:T(8,128)} fusion(f32[64,256,16]{1,2,0:T(8,128)} %fusion.26, f32[64,256,16]{1,2,0:T(8,128)S(1)} %copy-done.17, f32[64,512]{1,0:T(8,128)S(1)} %get-tuple-element.37, s32[64]{0:T(128)S(1)} %add_add_fusion, s32[256,512]{1,0:T(8,128)S(1)} %copy-done.6, f32[64,512]{1,0:T(8,128)S(1)} %copy-done.8, ...), kind=kOutput, calls=%fused_computation.53 | convolution fusion | flops 336330752 | bytes 4981248 | tf_op jit(solution)/shard_map/jan,njg->jag/dot_general | solution.py:94
  (79 shorter events, 41.6 us)
Async XLA Ops:
  7.2 8.0 copy-start.2
  7.2 7.9 copy-start.15
  10.2 39.0 %collective-permute-start = (bf16[64,2048,3]{1,0,2:T(8,128)(2,1)S(1)}, bf16[64,2048,3]{1,0,2:T(8,128)(2,1)S(1)}, u32[]{:S(2)}, u32[]{:S(2)}) collective-permute-start(bf16[64,2048,3]{1,0,2:T(8,128)(2,1)S(1)} %copy.126), channel_id=1, source_target_pairs={{0,2},{1,3},{4,6},{5,7},{8,10},{9,11},{12,14},{13,15},{16,18},{17,... | collective-permute-start | bytes 2359304 | tf_op jit(solution)/shard_map/ppermute | solution.py:19
  155.9 7.7 copy-start.3
  158.5 5.3 copy-start.9
  158.5 87.3 %all-to-all-start = ((bf16[8,2,32768]{2,1,0:T(2,128)(2,1)}), bf16[8,2,32768]{2,1,0:T(2,128)(2,1)S(1)}, u32[]{:S(2)}, u32[]{:S(2)}) async-start(bf16[8,2,32768]{2,1,0:T(2,128)(2,1)} %reshape.179), calls=%async_computation | async-start | bytes 2097152 | tf_op jit(solution)/shard_map/all_to_all | solution.py:127
  163.5 122.7 %all-gather.2.cloned.1.call-start = ((), (), s32[]{:S(2)}) async-start(), calls=%async_computation.1 | async-start | bytes 6291456 | tf_op jit(solution)/shard_map/all_gather | solution.py:132
  164.5 0.6 copy-start.7
  211.2 33.5 %copy-start.16 = (s32[2,256]{1,0:T(2,128)S(1)}, s32[2,256]{1,0:T(2,128)}, u32[]{:S(2)}) copy-start(s32[2,256]{1,0:T(2,128)} %param.10) | copy-start | bytes 6148
  256.0 0.9 copy-start.13
  286.2 7.9 copy-start.5
  286.2 7.9 copy-start.8
  294.1 254.0 %copy-start = (bf16[4,128,64,2,2,8]{1,5,0,4,2,3:T(8,128)(2,1)}, bf16[4,128,64,2,2,8]{1,5,0,4,2,3:T(8,128)(2,1)S(1)}, u32[]{:S(2)}) copy-start(bf16[4,128,64,2,2,8]{1,5,0,4,2,3:T(8,128)(2,1)S(1)} %copy.133) | copy-start | bytes 6291460
  572.8 44.6 %copy-start.1 = (bf16[4,128,64,2,2,8]{1,5,0,4,2,3:T(8,128)(2,1)S(1)}, bf16[4,128,64,2,2,8]{1,5,0,4,2,3:T(8,128)(2,1)}, u32[]{:S(2)}) copy-start(bf16[4,128,64,2,2,8]{1,5,0,4,2,3:T(8,128)(2,1)} %copy-done) | copy-start | bytes 6291460
  572.8 44.6 %copy-start.6 = (s32[256,512]{1,0:T(8,128)S(1)}, s32[256,512]{1,0:T(8,128)}, u32[]{:S(2)}) copy-start(s32[256,512]{1,0:T(8,128)} %add_select_fusion.1) | copy-start | bytes 1572868
  777.8 64.6 %copy-start.11 = (f32[64,512,1]{1,2,0:T(1,128)S(1)}, f32[64,512,1]{1,2,0:T(1,128)}, u32[]{:S(2)}) copy-start(f32[64,512,1]{1,2,0:T(1,128)} %copy.140) | copy-start | bytes 393220
  777.8 64.6 %copy-start.12 = (f32[64,512,1]{1,2,0:T(1,128)S(1)}, f32[64,512,1]{1,2,0:T(1,128)}, u32[]{:S(2)}) copy-start(f32[64,512,1]{1,2,0:T(1,128)} %stack.64) | copy-start | bytes 393220
  842.4 39.3 %copy-start.14 = (f32[64,1,256]{2,1,0:T(1,128)S(1)}, f32[64,1,256]{2,1,0:T(1,128)}, u32[]{:S(2)}) copy-start(f32[64,1,256]{2,1,0:T(1,128)} %fusion.5) | copy-start | bytes 196612
  842.4 39.4 %copy-start.4 = (f32[64,2,256]{2,1,0:T(2,128)S(1)}, f32[64,2,256]{2,1,0:T(2,128)}, u32[]{:S(2)}) copy-start(f32[64,2,256]{2,1,0:T(2,128)} %constant_dynamic-slice_fusion.1) | copy-start | bytes 393220
  842.4 41.4 %copy-start.10 = (s32[64,512]{1,0:T(8,128)S(1)}, s32[64,512]{1,0:T(8,128)}, u32[]{:S(2)}) copy-start(s32[64,512]{1,0:T(8,128)} %param.11) | copy-start | bytes 393220
  911.2 40.3 %copy-start.17 = (f32[64,256,16]{1,2,0:T(8,128)S(1)}, f32[64,256,16]{1,2,0:T(8,128)}, u32[]{:S(2)}) copy-start(f32[64,256,16]{1,2,0:T(8,128)} %fusion.10) | copy-start | bytes 3145732
Sparse Core Ops, SparseCore 0:
  256.1 15.0 all-gather.1
where the time goes:
time: 1100 us; the launch traced here: 1090 us
  matrix products  796 us (72%)
  other arithmetic  134 us (12%)
  local copies, waits for them, and re-layouts  130 us (12%)
  between operations  14.9 us (1%)
    dot_general x1, matrix products, form_beams(): jnp.einsum('jan,njg->jag', steering_imaginary, spectrum_imaginary, prefer...  128 us
    dot_general x1, matrix products, form_beams(): jnp.einsum('jan,njg->jag', steering_imaginary, spectrum_real, preferred_e...  128 us
    dot_general x1, matrix products, form_beams(): jnp.einsum('jan,njg->jag', steering_real, spectrum_imaginary, preferred_e...  127 us
    dot_general x1, matrix products, form_beams(): jnp.einsum('jan,njg->jag', steering_real, spectrum_real, preferred_elemen...  127 us
    unnamed x41, local copies, waits for them, and re-layouts  95.5 us
    dot_general x2, matrix products, shards(): jnp.einsum('csrj,cjv->csrv', weighted, vectors, precision=lax.Precision.H...  78.3 us
    add x1, other arithmetic, shards(): vis_used[:, 0] * model_values[:, 0] + vis_used[:, 1] * model_values[:, 1]  64.6 us
    dot_general x2, matrix products, matvec(): jnp.einsum('crj,cj->cr', matrix, vector, precision=lax.Precision.HIGHEST)  56.6 us
  transfers between devices with their start and end apart: 3, of which 0 were waited for; matrix products, arithmetic and copies ran while one was open for 13% of the time, Pallas kernels for 0%

commit v1 on v0

v1 whole, which is shorter than its diff:
```python
import functools
import math

import jax
import jax.numpy as jnp
from jax import lax
from jax.experimental import pallas as pl
from jax.experimental.pallas import tpu as pltpu
from jax.sharding import PartitionSpec as P

NCH = 512
ITERS = 2

damping = 0.5
epsilon = 1e-06
F32 = jnp.float32
BF16 = jnp.bfloat16


def from_behind(block, axis, distance):
    devices = range(lax.axis_size(axis))
    route = [(i - distance, i) for i in devices if i - distance in devices]
    return lax.ppermute(block, axis, route)


def unit_rows(rows, columns, transform_count):
    phases = (rows[:, None] * columns[None, :] % transform_count).astype(F32) * (
        2.0 * math.pi / transform_count
    )
    return jnp.cos(phases), jnp.sin(phases)


def transform_table(kept_count, transform_count):
    fine = 1 << ((kept_count.bit_length() - 1) // 2)
    coarse = kept_count // fine
    columns = jnp.arange(transform_count, dtype=jnp.int32)
    high_c, high_s = unit_rows(jnp.arange(coarse, dtype=jnp.int32) * fine, columns, transform_count)
    low_c, low_s = unit_rows(jnp.arange(fine, dtype=jnp.int32), columns, transform_count)
    high_c, high_s, low_c, low_s = lax.optimization_barrier((high_c, high_s, low_c, low_s))
    scale = 1.0 / math.sqrt(transform_count)
    high_c, high_s = high_c * scale, high_s * scale
    cosine = high_c[:, None] * low_c[None] - high_s[:, None] * low_s[None]
    sine = high_s[:, None] * low_c[None] + high_c[:, None] * low_s[None]
    cosine = cosine.reshape(kept_count, transform_count).astype(BF16)
    sine = sine.reshape(kept_count, transform_count).astype(BF16)
    real_row = jnp.concatenate([cosine, sine], axis=1)
    imag_row = jnp.concatenate([-sine, cosine], axis=1)
    return real_row, imag_row


def filter_bank(samples, window_taps, kept_count):
    local_inputs, _, transform_count, frames = samples.shape
    tap_count = window_taps.shape[0]
    framed = jnp.transpose(samples, (3, 0, 1, 2))
    previous = from_behind(framed[frames - tap_count + 1 :], "tm", 1)
    extended = jnp.concatenate([previous, framed], axis=0).astype(F32)
    windowed = sum(
        extended[tap : tap + frames] * window_taps[tap][None, None, None, :]
        for tap in range(tap_count)
    )
    windowed = windowed.astype(BF16).reshape(frames * local_inputs, 2 * transform_count)
    tables = transform_table(kept_count, transform_count)
    parts = [
        lax.dot_general(t, windowed, (((1,), (1,)), ((), ())), preferred_element_type=F32)
        for t in tables
    ]
    return jnp.stack([p.astype(BF16) for p in parts], axis=1)


NT = (((1,), (1,)), ((), ()))
TN = (((0,), (0,)), ((), ()))


def dot_nt(a, b):
    return lax.dot_general(a, b, NT, preferred_element_type=F32)


def gain_update(x, own, model, gains, older, flags):
    half = x.shape[0] // 2
    frames = half
    hr, hi = gains[0:1] * flags, gains[1:2] * flags
    xr, xi = x[:half].astype(F32), x[half:].astype(F32)
    y = jnp.concatenate([xr * hr + xi * hi, xi * hr - xr * hi], axis=0).astype(BF16)
    a = dot_nt(y, model[0])
    b = dot_nt(y, model[1])
    zr = a[:half] - b[half:]
    zi = a[half:] + b[:half]
    pr, pi = own[:half].astype(F32), own[half:].astype(F32)
    numer_r = jnp.sum(pr * zr + pi * zi, axis=0, keepdims=True) * (1.0 / frames)
    numer_i = jnp.sum(pi * zr - pr * zi, axis=0, keepdims=True) * (1.0 / frames)
    power = flags * (gains[0:1] * gains[0:1] + gains[1:2] * gains[1:2])
    top = power.astype(BF16)
    rest = (power - top.astype(F32)).astype(BF16)
    mr, mi = model[0].astype(F32), model[1].astype(F32)
    model_power = (mr * mr + mi * mi).astype(BF16)
    both = jnp.concatenate(
        [jnp.broadcast_to(top.astype(F32), (8, top.shape[1])),
         jnp.broadcast_to(rest.astype(F32), (8, top.shape[1]))], axis=0
    ).astype(BF16)
    d = dot_nt(both, model_power)
    denom = d[0:1] + d[8:9] + epsilon
    update = jnp.concatenate([numer_r, numer_i], axis=0) / denom
    return damping * older + (1.0 - damping) * update


def correlate_kernel(beam_ref, x_ref, own_ref, model_ref, gain_ref, older_ref, flag_ref, vis_ref, new_ref):
    for c in range(x_ref.shape[0]):
        x, own = x_ref[c], own_ref[c]
        half = x.shape[0] // 2
        scale = 1.0 / half
        vis_ref[c, 0] = (
            lax.dot_general(own, x, TN, preferred_element_type=F32) * scale
        ).astype(BF16)
        rotated = jnp.concatenate([own[half:], -own[:half]], axis=0)
        vis_ref[c, 1] = (
            lax.dot_general(rotated, x, TN, preferred_element_type=F32) * scale
        ).astype(BF16)
        new_ref[c] = gain_update(
            x, own, model_ref.at[c], gain_ref[c], older_ref[c], flag_ref[c].astype(F32)
        )


def update_kernel(beam_ref, x_ref, own_ref, model_ref, gain_ref, older_ref, flag_ref, new_ref):
    for c in range(x_ref.shape[0]):
        new_ref[c] = gain_update(
            x_ref[c], own_ref[c], model_ref.at[c], gain_ref[c], older_ref[c],
            flag_ref[c].astype(F32),
        )


def gain_call(correlate, beam_index, x, model, gains, older, flags):
    channels, rows, inputs = x.shape
    mine = model.shape[2]
    block = math.gcd(channels, 4)
    whole = lambda *shape: pl.BlockSpec((block, *shape), lambda c, b: (c,) + (0,) * len(shape))
    part = lambda r: pl.BlockSpec((block, r, mine), lambda c, b: (c, 0, b[0]))
    older_spec = part(2) if older.shape[2] == inputs else whole(2, mine)
    new_shape = jax.ShapeDtypeStruct((channels, 2, mine), F32)
    if correlate:
        out_shape = [jax.ShapeDtypeStruct(model.shape, BF16), new_shape]
        out_specs = [whole(2, mine, inputs), whole(2, mine)]
    else:
        out_shape, out_specs = new_shape, whole(2, mine)
    return pl.pallas_call(
        correlate_kernel if correlate else update_kernel,
        out_shape=out_shape,
        grid_spec=pltpu.PrefetchScalarGridSpec(
            num_scalar_prefetch=1,
            grid=(channels // block,),
            in_specs=[whole(rows, inputs), part(rows), whole(2, mine, inputs), whole(2, inputs),
                      older_spec, whole(1, inputs)],
            out_specs=out_specs,
        ),
        cost_estimate=pl.CostEstimate(
            flops=8 * channels * mine * inputs * rows,
            bytes_accessed=(4 + 4 * correlate) * model.size // 2,
            transcendentals=0,
        ),
        name="correlate" if correlate else "update",
    )(beam_index, x, x, model, gains, older, flags)


def beam_kernel(base_ref, x_ref, gain_ref, flag_ref, bits_ref, power_ref, cur_r, cur_i, one_r, one_i, rot_r, rot_i, *, unit, scale):
    block = x_ref.shape[0]
    beams, inputs = cur_r.shape
    step = 16

    @pl.when(pl.program_id(0) == 0)
    def _():
        first = base_ref[0]

        def fill(r, carry):
            rows = pl.ds(r * 8, 8)
            bits = bits_ref[rows, :]
            angle = (bits * first).astype(F32) * unit
            cur_r[rows, :] = jnp.cos(angle)
            cur_i[rows, :] = jnp.sin(angle)
            small = bits.astype(F32) * unit
            one_r[rows, :] = jnp.cos(small)
            one_i[rows, :] = jnp.sin(small)
            return carry

        lax.fori_loop(0, beams // 8, fill, 0)

    def turn(r, carry):
        rows = pl.ds(r * step, step)
        ar, ai = cur_r[rows, :], cur_i[rows, :]
        br, bi = one_r[rows, :], one_i[rows, :]
        for c in range(block):
            rot_r[c, rows, :] = ar.astype(BF16)
            rot_i[c, rows, :] = ai.astype(BF16)
            ar, ai = ar * br - ai * bi, ar * bi + ai * br
        cur_r[rows, :] = ar
        cur_i[rows, :] = ai
        return carry

    lax.fori_loop(0, beams // step, turn, 0)
    for c in range(block):
        x, gains = x_ref[c], gain_ref[c]
        flags = flag_ref[c].astype(F32) * scale
        half = x.shape[0] // 2
        hr, hi = gains[0:1] * flags, gains[1:2] * flags
        xr, xi = x[:half].astype(F32), x[half:].astype(F32)
        y = jnp.concatenate([xr * hr - xi * hi, xi * hr + xr * hi], axis=0)
        top = y.astype(BF16)
        rest = (y - top.astype(F32)).astype(BF16)
        both = jnp.concatenate([top, rest], axis=0)
        a = dot_nt(both, rot_r[c])
        b = dot_nt(both, rot_i[c])
        a = a[: 2 * half] + a[2 * half :]
        b = b[: 2 * half] + b[2 * half :]
        vr = a[:half] - b[half:]
        vi = a[half:] + b[:half]
        power_ref[c] = vr * vr + vi * vi


def form_beams(x, gains, flags, beam_steering, first_channel, chan_total):
    channels, rows, inputs = x.shape
    beams = beam_steering.shape[1]
    positions = jnp.arange(inputs, dtype=jnp.int32)
    column = positions // (inputs // 4)
    within = positions % (inputs // 4)
    bits = (
        beam_steering[0][:, None] * column[None, :] * 64
        + beam_steering[1][:, None] * within[None, :]
    ) % 256
    block = math.gcd(channels, 8)
    whole = lambda *shape: pl.BlockSpec((block, *shape), lambda c, b: (c,) + (0,) * len(shape))
    kernel = functools.partial(
        beam_kernel, unit=2.0 * math.pi / (512 * chan_total), scale=1.0 / math.sqrt(inputs)
    )
    return pl.pallas_call(
        kernel,
        out_shape=jax.ShapeDtypeStruct((channels, rows // 2, beams), F32),
        grid_spec=pltpu.PrefetchScalarGridSpec(
            num_scalar_prefetch=1,
            grid=(channels // block,),
            in_specs=[whole(rows, inputs), whole(2, inputs), whole(1, inputs),
                      pl.BlockSpec((beams, inputs), lambda c, b: (0, 0))],
            out_specs=whole(rows // 2, beams),
            scratch_shapes=[pltpu.VMEM((beams, inputs), F32)] * 4
            + [pltpu.VMEM((block, beams, inputs), BF16)] * 2,
        ),
        cost_estimate=pl.CostEstimate(
            flops=8 * channels * beams * inputs * rows,
            bytes_accessed=2 * x.size * 20,
            transcendentals=0,
        ),
        name="beams",
    )(jnp.reshape(chan_total + first_channel, (1,)), x, gains, flags, bits)


def shards(samples, window_taps, sky_model, prior_gains, beam_steering, input_flags):
    local_inputs = samples.shape[0]
    frames = samples.shape[3]
    kept_count = NCH
    time_count = lax.axis_size("tm")
    chan_count = lax.axis_size("chan")
    beam_count = lax.axis_size("beam")
    owners = time_count * chan_count
    chan_local = kept_count // owners
    spectra = filter_bank(samples, window_taps, kept_count)
    spectra = spectra.reshape(owners, chan_local, 2, frames * local_inputs)
    mixed = lax.all_to_all(spectra, ("chan", "tm"), split_axis=0, concat_axis=0, tiled=True)
    joined = lax.all_gather(mixed, "beam", axis=0)
    joined = joined.reshape(
        beam_count, chan_count, time_count, chan_local, 2, frames, local_inputs
    )
    x = jnp.transpose(joined, (3, 4, 2, 5, 1, 0, 6)).reshape(
        chan_local, 2 * time_count * frames, chan_count * beam_count * local_inputs
    )
    flags = input_flags[:, None, :]
    beam_index = jnp.reshape(lax.axis_index("beam"), (1,)).astype(jnp.int32)
    visibilities, updated = gain_call(
        True, beam_index, x, sky_model, prior_gains, prior_gains, flags
    )
    first_channel = (lax.axis_index("chan") * time_count + lax.axis_index("tm")) * chan_local
    beam_power = form_beams(
        x, prior_gains, flags, beam_steering, first_channel.astype(jnp.int32), kept_count
    )
    for _ in range(ITERS - 1):
        current = lax.all_gather(updated, "beam", axis=2, tiled=True)
        updated = gain_call(False, beam_index, x, sky_model, current, updated, flags)
    return (visibilities, updated, jnp.transpose(beam_power, (0, 2, 1)))


def solution(mesh):
    return jax.shard_map(
        shards,
        mesh=mesh,
        in_specs=(
            P(("group", "chan", "beam"), None, None, "tm"),
            P(),
            P(("group", "chan", "tm"), None, "beam", None),
            P(("group", "chan", "tm"), None, None),
            P(None, ("group", "beam")),
            P(("group", "chan", "tm"), None),
        ),
        out_specs=(
            P(("group", "chan", "tm"), None, "beam", None),
            P(("group", "chan", "tm"), None, "beam"),
            P(("group", "chan", "tm"), "beam", None),
        ),
        check_vma=False,
    )
```

time: 1100 us -> 203 us (0.18); the launches traced: 1090 us -> 202 us
  matrix products: 796 us -> 2.75 us
  other arithmetic: 134 us -> 5.67 us
  local copies, waits for them, and re-layouts: 130 us -> 33.1 us
  Pallas kernels: 0 us -> 83.1 us
  blocking collectives: 1.99 us -> 35.4 us
  waiting for transfers between devices: 0.03 us -> 22.7 us
    dot_general x21 -> x2, matrix products: 761 us -> 2.75 us  [filter_bank(): lax.dot_general(t, windowed, (((1,), (1,)), ((), ())), preferred_element_...]
    unnamed x41 -> x8, local copies, waits for them, and re-layouts: 95.5 us -> 3.35 us
    pallas_call x0 -> x3, Pallas kernels: none -> 83.1 us  [the longest x2 57.3 us: gain_call(): pl.pallas_call(correlate_kernel if correlate else update_kernel, out_shap...]
    add x4 -> x0, other arithmetic: 64.6 us -> none  [the longest x1 64.6 us: shards(): vis_used[:, 0] * model_values[:, 0] + vis_used[:, 1] * model_values[:, 1]]
    convert_element_type x2 -> x3, other arithmetic: 65.5 us -> 3.4 us  [the longest x1 2.31 us: filter_bank(): windowed.astype(BF16).reshape(frames * local_inputs, 2 * transform_count)]
    unnamed x4 -> x0, matrix products: 34.1 us -> none
    all_to_all x0 -> x1, blocking collectives: none -> 31.8 us  [shards(): lax.all_to_all(spectra, ('chan', 'tm'), split_axis=0, concat_axis=0, tile...]
    reshape x0 -> x2, local copies, waits for them, and re-layouts: none -> 16.2 us  [the longest x1 10.1 us: shards(): jnp.transpose(joined, (3, 4, 2, 5, 1, 0, 6))]
  transfers between devices with their start and end apart: 3 -> 2, of which waited for: 0 -> 2; matrix products, arithmetic and copies ran while one was open for 13% -> 2% of each run, Pallas kernels for 0% -> 0%
where the time goes in v1:
time: 203 us; the launch traced here: 202 us
  Pallas kernels  83.1 us (41%)
  blocking collectives  35.4 us (17%)
  local copies, waits for them, and re-layouts  33.1 us (16%)
  waiting for transfers between devices  22.7 us (11%)
  between operations  14.2 us (7%)
  other arithmetic  5.67 us (3%)
  starting transfers between devices  4.96 us (2%)
  matrix products  2.75 us (1%)
    pallas_call x2, Pallas kernels, gain_call(): pl.pallas_call(correlate_kernel if correlate else update_kernel, out_shap...  57.3 us
    all_to_all x1, blocking collectives, shards(): lax.all_to_all(spectra, ('chan', 'tm'), split_axis=0, concat_axis=0, tile...  31.8 us
    pallas_call x1, Pallas kernels, form_beams(): pl.pallas_call(kernel, out_shape=jax.ShapeDtypeStruct((channels, rows //...  25.9 us
    ppermute x1, waiting for transfers between devices, from_behind(): return lax.ppermute(block, axis, route)  14.9 us
    transpose x1, local copies, waits for them, and re-layouts, shards(): jnp.transpose(joined, (3, 4, 2, 5, 1, 0, 6))  10.6 us
    reshape x1, local copies, waits for them, and re-layouts, shards(): jnp.transpose(joined, (3, 4, 2, 5, 1, 0, 6))  10.1 us
    all_gather x1, waiting for transfers between devices, shards(): joined = lax.all_gather(mixed, 'beam', axis=0)  7.82 us
    reshape x1, local copies, waits for them, and re-layouts, shards(): joined.reshape(beam_count, chan_count, time_count, chan_local, 2, frames,...  6.14 us
  transfers between devices with their start and end apart: 2, of which 2 were waited for; matrix products, arithmetic and copies ran while one was open for 2% of the time, Pallas kernels for 0%

profile of v1, /device:TPU:0, one launch (start us, length us, event | category | flops | bytes accessed | tf_op | source)
XLA Modules:
  0.0 202.0 jit_solution(17018785366574674083)
XLA Ops:
  7.2 0.0 all-gather.3.cloned.1.call-start
  7.2 2.7 %copy.20 = bf16[64,2,1024,8]{2,0,1,3:T(8,128)(2,1)S(1)} copy(bf16[64,2,1024,8]{2,3,1,0:T(8,128)(2,1)} %param.6) | data formatting | bytes 4194304 | tf_op args[0]
  10.0 0.0 copy-start.1
  10.0 0.1 slice.44
  10.0 4.9 %collective-permute-start = (bf16[3,64,2,1024]{3,1,2,0:T(8,128)(2,1)S(1)}, bf16[3,64,2,1024]{3,1,2,0:T(8,128)(2,1)S(1)}, u32[]{:S(2)}, u32[]{:S(2)}) collective-permute-start(bf16[3,64,2,1024]{3,1,2,0:T(8,128)(2,1)S(1)} %slice.44), channel_id=1, source_target_pairs={{0,2},{1,3},{4,6},{5,7},{8,10},{9,11},{12,14},{13,15},{16,18},{17,... | collective-permute-start | bytes 2359304 | tf_op jit(solution)/shard_map/ppermute | solution.py:23
  15.0 0.3 fusion.33
  15.2 0.6 fusion.30
  15.9 0.0 copy-done.1
  15.9 0.7 add_convert_fusion
  16.6 0.1 bitcast_negate_fusion
  16.8 14.9 %collective-permute-done = bf16[3,64,2,1024]{3,1,2,0:T(8,128)(2,1)S(1)} collective-permute-done((bf16[3,64,2,1024]{3,1,2,0:T(8,128)(2,1)S(1)}, bf16[3,64,2,1024]{3,1,2,0:T(8,128)(2,1)S(1)}, u32[]{:S(2)}, u32[]{:S(2)}) %collective-permute-start) | collective-permute-done | bytes 786464 | tf_op jit(solution)/shard_map/ppermute | solution.py:23
  31.7 0.4 maximum_convert_fusion
  32.1 2.3 %fusion.1 = bf16[8,64,2,1024]{3,1,2,0:T(8,128)(2,1)S(1)} fusion(f32[11,64,2,1024]{3,1,2,0:T(8,128)S(1)} %maximum_convert_fusion, f32[1024]{0:T(1024)S(1)} %bitcast.44, f32[1024]{0:T(1024)S(1)} %bitcast.45, f32[1024]{0:T(1024)S(1)} %bitcast.43, f32[1024]{0:T(1024)S(1)} %bitcast.42), kind=kLoop, calls=%fused_computation.2 | loop fusion | flops 8388608 | bytes 18890752 | tf_op jit(solution)/shard_map/convert_element_type | solution.py:61
  34.4 2.2 %copy.14 = bf16[8,64,2,1024]{3,2,1,0:T(2,128)(2,1)S(1)} copy(bf16[8,64,2,1024]{3,1,2,0:T(8,128)(2,1)S(1)} %fusion.1) | data formatting | bytes 4194304 | tf_op jit(solution)/shard_map/convert_element_type | solution.py:61
  36.5 0.6 copy.18
  37.1 1.4 fusion.12
  38.5 1.4 fusion.15
  39.9 0.1 pad_maximum_fusion
  40.0 0.0 copy-start
  40.0 0.0 copy-start.2
  40.0 31.8 %all_to_all.5 = bf16[8,64,2,512]{3,1,2,0:T(8,128)(2,1)} all-to-all(bf16[8,64,2,512]{3,1,2,0:T(8,128)(2,1)S(1)} %pad_maximum_fusion), channel_id=1, replica_groups=mesh['group'=2,'chan'=4,'tm'=2,'beam'=2] {'chan','tm'}, dimensions={0} | all-to-all | bytes 2097152 | tf_op jit(solution)/shard_map/all_to_all | solution.py:264
  71.8 0.0 all-gather.3.cloned.1.call-update
  71.9 0.7 broadcast_in_dim.2.flag_ref
  72.6 1.1 add_select_fusion.bits_ref
  73.7 7.8 %all-gather.3.cloned.1.call-done = bf16[16,64,2,512]{3,1,2,0:T(8,128)(2,1)} async-done(((bf16[8,64,2,512]{3,1,2,0:T(8,128)(2,1)}), bf16[16,64,2,512]{3,1,2,0:T(8,128)(2,1)}) %all-gather.3.cloned.1.call-update) | async-done | bytes 2097168 | tf_op jit(solution)/shard_map/all_gather | solution.py:265
  81.6 6.1 %reshape.82 = bf16[2,4,2,64,2,8,64]{6,5,3,4,2,1,0:T(8,128)(2,1)} reshape(bf16[16,64,2,512]{3,1,2,0:T(8,128)(2,1)} %all-gather.3.cloned.1.call-done) | data formatting | bytes 4194304 | tf_op jit(solution)/shard_map/reshape | solution.py:266
  87.7 10.6 %copy.17 = bf16[64,2,2,8,4,2,64]{6,5,4,3,2,1,0:T(2,128)(2,1)} copy(bf16[64,2,2,8,4,2,64]{6,3,0,1,2,4,5:T(8,128)(2,1)} %bitcast.31) | data formatting | bytes 4194304 | tf_op jit(solution)/shard_map/transpose | solution.py:269
  98.3 10.1 %reshape.83.x_ref.own_ref = bf16[64,32,512]{2,1,0:T(8,128)(2,1)} reshape(bf16[64,2,2,8,4,2,64]{6,5,4,3,2,1,0:T(2,128)(2,1)} %copy.17) | data formatting | bytes 4194304 | tf_op jit(solution)/shard_map/reshape | solution.py:269
  108.4 33.4 %correlate.1 = (bf16[64,2,256,512]{3,2,1,0:T(8,128)(2,1)}, f32[64,2,256]{2,1,0:T(2,128)}) custom-call(s32[1]{0:T(128)} %bitcast.beam_ref, bf16[64,32,512]{2,1,0:T(8,128)(2,1)} %reshape.83.x_ref.own_ref, bf16[64,32,512]{2,1,0:T(8,128)(2,1)} %reshape.83.x_ref.own_ref, bf16[64,2,256,512]{3,2,1,0:T(8,128)(2,1)} %model_ref.3, f32[64,2,512]{2,1,0:T(2,128)} %gain_ref.3, ...), custom_call_target="tpu_custom_call" | custom-call | flops 2147483648 | bytes 67108864 | tf_op jit(solution)/shard_map/correlate/pallas_call | solution.py:144
  141.8 3.6 %all_gather.11.gain_ref = f32[64,2,512]{2,1,0:T(2,128)} all-gather(f32[64,2,256]{2,1,0:T(2,128)} %get-tuple-element.14.older_ref), channel_id=1, replica_groups=mesh['group'=2,'chan'=4,'tm'=2,'beam'=2] {'beam'}, dimensions={2}, use_global_device_ids=true | all-gather | bytes 393216 | tf_op jit(solution)/shard_map/all_gather | solution.py:282
  145.4 23.9 %update.1 = f32[64,2,256]{2,1,0:T(2,128)} custom-call(s32[1]{0:T(128)} %bitcast.beam_ref, bf16[64,32,512]{2,1,0:T(8,128)(2,1)} %reshape.83.x_ref.own_ref, bf16[64,32,512]{2,1,0:T(8,128)(2,1)} %reshape.83.x_ref.own_ref, bf16[64,2,256,512]{3,2,1,0:T(8,128)(2,1)} %model_ref.3, f32[64,2,512]{2,1,0:T(2,128)} %all_gather.11.gain_ref, ...), custom_call_target="tpu_custom_call" | custom-call | flops 2147483648 | bytes 33554432 | tf_op jit(solution)/shard_map/update/pallas_call | solution.py:144
  169.3 25.9 %beams.1 = f32[64,16,256]{2,1,0:T(8,128)} custom-call(s32[1]{0:T(128)} %bitcast.13.base_ref, bf16[64,32,512]{2,1,0:T(8,128)(2,1)} %reshape.83.x_ref.own_ref, f32[64,2,512]{2,1,0:T(2,128)} %gain_ref.3, s32[64,1,512]{2,1,0:T(1,128)} %broadcast_in_dim.2.flag_ref, s32[256,512]{1,0:T(8,128)} %add_select_fusion.bits_ref), custom_call_target="tpu_custom_call" | custom-call | flops 2147483648 | bytes 41943040 | tf_op jit(solution)/shard_map/beams/pallas_call | solution.py:232
  (8 shorter events, 0.1 us)
Async XLA Ops:
  7.2 74.4 %all-gather.3.cloned.1.call-start = ((), (), s32[]{:S(2)}) async-start(), calls=%async_computation.1 | async-start | bytes 3145728 | tf_op jit(solution)/shard_map/all_gather | solution.py:265
  10.0 5.9 %copy-start.1 = (f32[4,1024]{1,0:T(4,128)S(1)}, f32[4,1024]{1,0:T(4,128)}, u32[]{:S(2)}) copy-start(f32[4,1024]{1,0:T(4,128)} %param.7) | copy-start | bytes 49156
  10.0 21.7 %collective-permute-start = (bf16[3,64,2,1024]{3,1,2,0:T(8,128)(2,1)S(1)}, bf16[3,64,2,1024]{3,1,2,0:T(8,128)(2,1)S(1)}, u32[]{:S(2)}, u32[]{:S(2)}) collective-permute-start(bf16[3,64,2,1024]{3,1,2,0:T(8,128)(2,1)S(1)} %slice.44), channel_id=1, source_target_pairs={{0,2},{1,3},{4,6},{5,7},{8,10},{9,11},{12,14},{13,15},{16,18},{17,... | collective-permute-start | bytes 2359304 | tf_op jit(solution)/shard_map/ppermute | solution.py:23
  40.0 31.9 %copy-start = (s32[64,512]{1,0:T(8,128)S(1)}, s32[64,512]{1,0:T(8,128)}, u32[]{:S(2)}) copy-start(s32[64,512]{1,0:T(8,128)} %param.11) | copy-start | bytes 393220
  40.0 32.6 %copy-start.2 = (s32[2,256]{1,0:T(2,128)S(1)}, s32[2,256]{1,0:T(2,128)}, u32[]{:S(2)}) copy-start(s32[2,256]{1,0:T(2,128)} %param.10) | copy-start | bytes 6148
Sparse Core Ops, SparseCore 0:
  72.0 9.5 all-gather.2

commit v2 on v1

v2 whole, which is shorter than its diff:
```python
import functools
import math

import jax
import jax.numpy as jnp
from jax import lax
from jax.experimental import pallas as pl
from jax.experimental.pallas import tpu as pltpu
from jax.sharding import PartitionSpec as P

NCH = 512
ITERS = 2

damping = 0.5
epsilon = 1e-06
F32 = jnp.float32
BF16 = jnp.bfloat16


def from_behind(block, axis, distance):
    devices = range(lax.axis_size(axis))
    route = [(i - distance, i) for i in devices if i - distance in devices]
    return lax.ppermute(block, axis, route)


def unit_rows(rows, columns, transform_count):
    phases = (rows[:, None] * columns[None, :] % transform_count).astype(F32) * (
        2.0 * math.pi / transform_count
    )
    return jnp.cos(phases), jnp.sin(phases)


def transform_table(kept_count, transform_count):
    fine = 1 << ((kept_count.bit_length() - 1) // 2)
    coarse = kept_count // fine
    columns = jnp.arange(transform_count, dtype=jnp.int32)
    high_c, high_s = unit_rows(jnp.arange(coarse, dtype=jnp.int32) * fine, columns, transform_count)
    low_c, low_s = unit_rows(jnp.arange(fine, dtype=jnp.int32), columns, transform_count)
    high_c, high_s, low_c, low_s = lax.optimization_barrier((high_c, high_s, low_c, low_s))
    scale = 1.0 / math.sqrt(transform_count)
    high_c, high_s = high_c * scale, high_s * scale
    cosine = high_c[:, None] * low_c[None] - high_s[:, None] * low_s[None]
    sine = high_s[:, None] * low_c[None] + high_c[:, None] * low_s[None]
    cosine = cosine.reshape(kept_count, transform_count).astype(BF16)
    sine = sine.reshape(kept_count, transform_count).astype(BF16)
    return cosine, sine


def filter_bank(samples, window_taps, kept_count, beside):
    local_inputs, _, transform_count, frames = samples.shape
    tap_count = window_taps.shape[0]
    framed = jnp.transpose(samples, (3, 1, 0, 2))
    previous = from_behind(framed[frames - tap_count + 1 :], "tm", 1)
    previous, beside = lax.optimization_barrier((previous, beside))
    extended = jnp.concatenate([previous, framed], axis=0).astype(F32)
    windowed = sum(
        extended[tap : tap + frames] * window_taps[tap][None, None, None, :]
        for tap in range(tap_count)
    )
    windowed = windowed.astype(BF16)
    real_in = windowed[:, 0].reshape(frames * local_inputs, transform_count)
    imag_in = windowed[:, 1].reshape(frames * local_inputs, transform_count)
    cosine, sine = transform_table(kept_count, transform_count)
    real = dot_nt(cosine, real_in) + dot_nt(sine, imag_in)
    imag = dot_nt(cosine, imag_in) - dot_nt(sine, real_in)
    return real.astype(BF16), imag.astype(BF16), beside


NT = (((1,), (1,)), ((), ()))
TN = (((0,), (0,)), ((), ()))


def dot_nt(a, b):
    return lax.dot_general(a, b, NT, preferred_element_type=F32)


def numerators(x, own, model, gains, flags):
    half = x.shape[0] // 2
    hr, hi = gains[0:1] * flags, gains[1:2] * flags
    xr, xi = x[:half].astype(F32), x[half:].astype(F32)
    y = jnp.concatenate([xr * hr + xi * hi, xi * hr - xr * hi], axis=0).astype(BF16)
    a = dot_nt(y, model[0])
    b = dot_nt(y, model[1])
    zr = a[:half] - b[half:]
    zi = a[half:] + b[:half]
    pr, pi = own[:half].astype(F32), own[half:].astype(F32)
    numer_r = jnp.sum(pr * zr + pi * zi, axis=0, keepdims=True) * (1.0 / half)
    numer_i = jnp.sum(pi * zr - pr * zi, axis=0, keepdims=True) * (1.0 / half)
    return jnp.concatenate([numer_r, numer_i], axis=0)


def denominators(model, gains, flags):
    power = flags * (gains[0:1] * gains[0:1] + gains[1:2] * gains[1:2])
    top = power.astype(BF16).astype(F32)
    wide = (8, top.shape[1])
    both = jnp.concatenate(
        [jnp.broadcast_to(top, wide), jnp.broadcast_to(power - top, wide)], axis=0
    ).astype(BF16)
    mr, mi = model[0].astype(F32), model[1].astype(F32)
    d = dot_nt(both, (mr * mr + mi * mi).astype(BF16))
    return d[0:1] + d[8:9] + epsilon


def damped(older, numer, denom):
    return damping * older + (1.0 - damping) * (numer / denom)


def denominator_kernel(model_ref, gain_ref, flag_ref, out_ref):
    for c in range(model_ref.shape[0]):
        out_ref[c] = denominators(model_ref.at[c], gain_ref[c], flag_ref[c].astype(F32))


def first_denominators(model, gains, flags):
    channels, _, mine, inputs = model.shape
    block = math.gcd(channels, 4)
    whole = lambda *shape: pl.BlockSpec((block, *shape), lambda c: (c,) + (0,) * len(shape))
    return pl.pallas_call(
        denominator_kernel,
        out_shape=jax.ShapeDtypeStruct((channels, 1, mine), F32),
        grid=(channels // block,),
        in_specs=[whole(2, mine, inputs), whole(2, inputs), whole(1, inputs)],
        out_specs=whole(1, mine),
        cost_estimate=pl.CostEstimate(
            flops=16 * model.size, bytes_accessed=2 * model.size, transcendentals=0
        ),
        name="denominators",
    )(model, gains, flags)


def correlate_kernel(beam_ref, x_ref, own_ref, model_ref, gain_ref, older_ref, flag_ref, denom_ref, vis_ref, new_ref):
    for c in range(x_ref.shape[0]):
        x, own = x_ref[c], own_ref[c]
        half = x.shape[0] // 2
        scale = 1.0 / half
        vis_ref[c, 0] = (
            lax.dot_general(own, x, TN, preferred_element_type=F32) * scale
        ).astype(BF16)
        rotated = jnp.concatenate([own[half:], -own[:half]], axis=0)
        vis_ref[c, 1] = (
            lax.dot_general(rotated, x, TN, preferred_element_type=F32) * scale
        ).astype(BF16)
        numer = numerators(x, own, model_ref.at[c], gain_ref[c], flag_ref[c].astype(F32))
        new_ref[c] = damped(older_ref[c], numer, denom_ref[c])


def update_kernel(beam_ref, x_ref, own_ref, model_ref, gain_ref, older_ref, flag_ref, new_ref):
    for c in range(x_ref.shape[0]):
        model, gains, flags = model_ref.at[c], gain_ref[c], flag_ref[c].astype(F32)
        numer = numerators(x_ref[c], own_ref[c], model, gains, flags)
        new_ref[c] = damped(older_ref[c], numer, denominators(model, gains, flags))


def turn_kernel(in_ref, out_ref, rows_ref, *, inputs):
    beams, chans, times, paired, lanes = in_ref.shape
    frames = lanes // inputs
    planes = times * frames
    width = rows_ref.shape[2]
    for b in range(beams):
        for z in range(chans):
            column = (z * beams + b) * inputs
            at = column % width
            for t in range(times):
                slab = in_ref[b, z, t].astype(F32)
                for f in range(frames):
                    plane = t * frames + f
                    rows_ref[
                        column // width, plane * paired : (plane + 1) * paired, at : at + inputs
                    ] = slab[:, f * inputs : (f + 1) * inputs]

    def gather(k, carry):
        for q in range(rows_ref.shape[0]):
            parts = [
                rows_ref.at[q][pl.ds(s * (paired // 2) + k, planes, stride=paired), :]
                for s in range(2)
            ]
            out_ref[k, :, q * width : (q + 1) * width] = jnp.concatenate(parts, axis=0).astype(BF16)
        return carry

    lax.fori_loop(0, paired // 2, gather, 0)


def turn(joined, inputs):
    beams, chans, times, paired, lanes = joined.shape
    planes = times * (lanes // inputs)
    total = chans * beams * inputs
    width = 128
    return pl.pallas_call(
        functools.partial(turn_kernel, inputs=inputs),
        out_shape=jax.ShapeDtypeStruct((paired // 2, 2 * planes, total), BF16),
        scratch_shapes=[pltpu.VMEM((total // width, planes * paired, width), F32)],
        cost_estimate=pl.CostEstimate(
            flops=0, bytes_accessed=8 * joined.size, transcendentals=0
        ),
        name="turn",
    )(joined)


def gain_call(beam_index, x, model, gains, older, flags, denom=None):
    correlate = denom is not None
    channels, rows, inputs = x.shape
    mine = model.shape[2]
    block = math.gcd(channels, 4)
    whole = lambda *shape: pl.BlockSpec((block, *shape), lambda c, b: (c,) + (0,) * len(shape))
    part = lambda r: pl.BlockSpec((block, r, mine), lambda c, b: (c, 0, b[0]))
    older_spec = part(2) if older.shape[2] == inputs else whole(2, mine)
    new_shape = jax.ShapeDtypeStruct((channels, 2, mine), F32)
    if correlate:
        out_shape = [jax.ShapeDtypeStruct(model.shape, BF16), new_shape]
        out_specs = [whole(2, mine, inputs), whole(2, mine)]
    else:
        out_shape, out_specs = new_shape, whole(2, mine)
    return pl.pallas_call(
        correlate_kernel if correlate else update_kernel,
        out_shape=out_shape,
        grid_spec=pltpu.PrefetchScalarGridSpec(
            num_scalar_prefetch=1,
            grid=(channels // block,),
            in_specs=[whole(rows, inputs), part(rows), whole(2, mine, inputs), whole(2, inputs),
                      older_spec, whole(1, inputs)] + [whole(1, mine)] * correlate,
            out_specs=out_specs,
        ),
        cost_estimate=pl.CostEstimate(
            flops=8 * channels * mine * inputs * rows,
            bytes_accessed=(4 + 4 * correlate) * model.size // 2,
            transcendentals=0,
        ),
        name="correlate" if correlate else "update",
    )(beam_index, x, x, model, gains, older, flags, *([denom] if correlate else []))


def steering_kernel(base_ref, bits_ref, rot_r, rot_i, cur_r, cur_i, one_r, one_i, *, unit):
    block = rot_r.shape[0]
    beams, inputs = cur_r.shape
    step = 16

    @pl.when(pl.program_id(0) == 0)
    def _():
        first = base_ref[0]

        def fill(r, carry):
            rows = pl.ds(r * 8, 8)
            bits = bits_ref[rows, :]
            angle = (bits * first).astype(F32) * unit
            cur_r[rows, :] = jnp.cos(angle)
            cur_i[rows, :] = jnp.sin(angle)
            small = bits.astype(F32) * unit
            one_r[rows, :] = jnp.cos(small)
            one_i[rows, :] = jnp.sin(small)
            return carry

        lax.fori_loop(0, beams // 8, fill, 0)

    def advance(r, carry):
        rows = pl.ds(r * step, step)
        ar, ai = cur_r[rows, :], cur_i[rows, :]
        br, bi = one_r[rows, :], one_i[rows, :]
        for c in range(block):
            rot_r[c, rows, :] = ar.astype(BF16)
            rot_i[c, rows, :] = ai.astype(BF16)
            ar, ai = ar * br - ai * bi, ar * bi + ai * br
        cur_r[rows, :] = ar
        cur_i[rows, :] = ai
        return carry

    lax.fori_loop(0, beams // step, advance, 0)


def steering(beam_steering, inputs, channels, first_channel, chan_total):
    beams = beam_steering.shape[1]
    positions = jnp.arange(inputs, dtype=jnp.int32)
    column = positions // (inputs // 4)
    within = positions % (inputs // 4)
    bits = (
        beam_steering[0][:, None] * column[None, :] * 64
        + beam_steering[1][:, None] * within[None, :]
    ) % 256
    block = math.gcd(channels, 8)
    rot = jax.ShapeDtypeStruct((channels, beams, inputs), BF16)
    rot_spec = pl.BlockSpec((block, beams, inputs), lambda c, b: (c, 0, 0))
    return pl.pallas_call(
        functools.partial(steering_kernel, unit=2.0 * math.pi / (512 * chan_total)),
        out_shape=[rot, rot],
        grid_spec=pltpu.PrefetchScalarGridSpec(
            num_scalar_prefetch=1,
            grid=(channels // block,),
            in_specs=[pl.BlockSpec((beams, inputs), lambda c, b: (0, 0))],
            out_specs=[rot_spec, rot_spec],
            scratch_shapes=[pltpu.VMEM((beams, inputs), F32)] * 4,
        ),
        cost_estimate=pl.CostEstimate(
            flops=8 * rot.size, bytes_accessed=6 * rot.size, transcendentals=0
        ),
        name="steering",
    )(jnp.reshape(chan_total + first_channel, (1,)), bits)


def beam_kernel(x_ref, gain_ref, flag_ref, rot_r, rot_i, power_ref, *, scale):
    for c in range(x_ref.shape[0]):
        x, gains = x_ref[c], gain_ref[c]
        flags = flag_ref[c].astype(F32) * scale
        half = x.shape[0] // 2
        hr, hi = gains[0:1] * flags, gains[1:2] * flags
        xr, xi = x[:half].astype(F32), x[half:].astype(F32)
        y = jnp.concatenate([xr * hr - xi * hi, xi * hr + xr * hi], axis=0)
        top = y.astype(BF16)
        rest = (y - top.astype(F32)).astype(BF16)
        both = jnp.concatenate([top, rest], axis=0)
        a = dot_nt(both, rot_r[c])
        b = dot_nt(both, rot_i[c])
        a = a[: 2 * half] + a[2 * half :]
        b = b[: 2 * half] + b[2 * half :]
        vr = a[:half] - b[half:]
        vi = a[half:] + b[:half]
        power_ref[c] = vr * vr + vi * vi


def form_beams(x, gains, flags, rot_r, rot_i):
    channels, rows, inputs = x.shape
    beams = rot_r.shape[1]
    block = math.gcd(channels, 4)
    whole = lambda *shape: pl.BlockSpec((block, *shape), lambda c: (c,) + (0,) * len(shape))
    return pl.pallas_call(
        functools.partial(beam_kernel, scale=1.0 / math.sqrt(inputs)),
        out_shape=jax.ShapeDtypeStruct((channels, rows // 2, beams), F32),
        grid=(channels // block,),
        in_specs=[whole(rows, inputs), whole(2, inputs), whole(1, inputs),
                  whole(beams, inputs), whole(beams, inputs)],
        out_specs=whole(rows // 2, beams),
        cost_estimate=pl.CostEstimate(
            flops=8 * channels * beams * inputs * rows,
            bytes_accessed=4 * rot_r.size, transcendentals=0,
        ),
        name="beams",
    )(x, gains, flags, rot_r, rot_i)


def shards(samples, window_taps, sky_model, prior_gains, beam_steering, input_flags):
    local_inputs = samples.shape[0]
    frames = samples.shape[3]
    kept_count = NCH
    time_count = lax.axis_size("tm")
    chan_count = lax.axis_size("chan")
    beam_count = lax.axis_size("beam")
    owners = time_count * chan_count
    chan_local = kept_count // owners
    first_channel = (lax.axis_index("chan") * time_count + lax.axis_index("tm")) * chan_local
    input_count = local_inputs * chan_count * beam_count
    rot_r, rot_i = steering(
        beam_steering, input_count, chan_local, first_channel.astype(jnp.int32), kept_count
    )
    flags = input_flags[:, None, :]
    denom = first_denominators(sky_model, prior_gains, flags)
    real, imag, (rot_r, rot_i) = filter_bank(samples, window_taps, kept_count, (rot_r, rot_i))
    by_owner = (owners, chan_local, frames * local_inputs)
    spectra = jnp.concatenate([real.reshape(by_owner), imag.reshape(by_owner)], axis=1)
    mixed = lax.all_to_all(spectra, ("chan", "tm"), split_axis=0, concat_axis=0, tiled=True)
    joined = lax.all_gather(mixed, "beam", axis=0)
    joined = joined.reshape(beam_count, chan_count, time_count, *joined.shape[2:])
    x = turn(joined, local_inputs)
    beam_index = jnp.reshape(lax.axis_index("beam"), (1,)).astype(jnp.int32)
    visibilities, updated = gain_call(
        beam_index, x, sky_model, prior_gains, prior_gains, flags, denom
    )
    beam_power = form_beams(x, prior_gains, flags, rot_r, rot_i)
    for _ in range(ITERS - 1):
        current = lax.all_gather(updated, "beam", axis=2, tiled=True)
        updated = gain_call(beam_index, x, sky_model, current, updated, flags)
    return (visibilities, updated, jnp.transpose(beam_power, (0, 2, 1)))


def solution(mesh):
    return jax.shard_map(
        shards,
        mesh=mesh,
        in_specs=(
            P(("group", "chan", "beam"), None, None, "tm"),
            P(),
            P(("group", "chan", "tm"), None, "beam", None),
            P(("group", "chan", "tm"), None, None),
            P(None, ("group", "beam")),
            P(("group", "chan", "tm"), None),
        ),
        out_specs=(
            P(("group", "chan", "tm"), None, "beam", None),
            P(("group", "chan", "tm"), None, "beam"),
            P(("group", "chan", "tm"), "beam", None),
        ),
        check_vma=False,
    )
```

time: 203 us -> 196 us (0.966)
  Pallas kernels: 83.1 us -> 128 us
  local copies, waits for them, and re-layouts: 33.1 us -> 4.64 us
  waiting for transfers between devices: 22.7 us -> 0.02 us
    pallas_call x1 -> x4, Pallas kernels: 25.9 us -> 68.7 us  [the longest x1 21.6 us: form_beams(): pl.pallas_call(functools.partial(beam_kernel, scale=1.0 / math.sqrt(input...]
    reshape x2 -> x0, local copies, waits for them, and re-layouts: 16.2 us -> none  [the longest x1 10.1 us: shards(): jnp.transpose(joined, (3, 4, 2, 5, 1, 0, 6))]
    ppermute x1, waiting for transfers between devices: 14.9 us -> 0.01 us  [from_behind(): return lax.ppermute(block, axis, route)]
    transpose x1 -> x0, local copies, waits for them, and re-layouts: 10.6 us -> none  [shards(): jnp.transpose(joined, (3, 4, 2, 5, 1, 0, 6))]
    all_gather x1, waiting for transfers between devices: 7.82 us -> 0.01 us  [shards(): joined = lax.all_gather(mixed, 'beam', axis=0)]
    pallas_call x2, Pallas kernels: 57.3 us -> 59.6 us  [gain_call(): pl.pallas_call(correlate_kernel if correlate else update_kernel, out_shap...]
    convert_element_type x1 -> x0, local copies, waits for them, and re-layouts: 2.16 us -> none  [filter_bank(): windowed.astype(BF16).reshape(frames * local_inputs, 2 * transform_count)]
  transfers between devices with their start and end apart: 2 -> 2, of which waited for: 2 -> 0; matrix products, arithmetic and copies ran while one was open for 2% -> 2% of each run, Pallas kernels for 0% -> 20%
where the time goes in v2:
time: 196 us; the launch traced here: 195 us
  Pallas kernels  128 us (65%)
  blocking collectives  33.9 us (17%)
  between operations  14.2 us (7%)
  other arithmetic  5.49 us (3%)
  starting transfers between devices  4.95 us (3%)
  local copies, waits for them, and re-layouts  4.64 us (2%)
  matrix products  3.14 us (2%)
    pallas_call x2, Pallas kernels, gain_call(): pl.pallas_call(correlate_kernel if correlate else update_kernel, out_shap...  59.6 us
    all_to_all x1, blocking collectives, shards(): lax.all_to_all(spectra, ('chan', 'tm'), split_axis=0, concat_axis=0, tile...  30.3 us
    pallas_call x1, Pallas kernels, form_beams(): pl.pallas_call(functools.partial(beam_kernel, scale=1.0 / math.sqrt(input...  21.6 us
    pallas_call x1, Pallas kernels, first_denominators(): pl.pallas_call(denominator_kernel, out_shape=jax.ShapeDtypeStruct((channe...  19.7 us
    pallas_call x1, Pallas kernels, steering(): pl.pallas_call(functools.partial(steering_kernel, unit=2.0 * math.pi / (5...  19.1 us
    pallas_call x1, Pallas kernels, turn(): pl.pallas_call(functools.partial(turn_kernel, inputs=inputs), out_shape=j...  8.32 us
    ppermute x1, starting transfers between devices, from_behind(): return lax.ppermute(block, axis, route)  4.91 us
  transfers between devices with their start and end apart: 2, of which 0 were waited for; matrix products, arithmetic and copies ran while one was open for 2% of the time, Pallas kernels for 20%

profile of v2, /device:TPU:0, one launch (start us, length us, event | category | flops | bytes accessed | tf_op | source)
XLA Modules:
  0.0 194.7 jit_solution(17766293318707705660)
XLA Ops:
  7.2 0.0 copy-start.2
  7.2 0.0 copy-start.1
  7.2 0.0 all-gather.3.cloned.1.call-start
  7.2 2.7 %copy.12 = bf16[64,2,1024,8]{2,0,3,1:T(8,128)(2,1)S(1)} copy(bf16[64,2,1024,8]{2,3,1,0:T(8,128)(2,1)} %param.6) | data formatting | bytes 4194304 | tf_op args[0]
  10.0 1.0 slice.52
  10.9 4.9 %collective-permute-start = (bf16[3,2,64,1024]{3,2,0,1:T(8,128)(2,1)}, bf16[3,2,64,1024]{3,2,0,1:T(8,128)(2,1)S(1)}, u32[]{:S(2)}, u32[]{:S(2)}) collective-permute-start(bf16[3,2,64,1024]{3,2,0,1:T(8,128)(2,1)} %slice.52), channel_id=1, source_target_pairs={{0,2},{1,3},{4,6},{5,7},{8,10},{9,11},{12,14},{13,15},{16,18},{17,... | collective-permute-start | bytes 2359304 | tf_op jit(solution)/shard_map/ppermute | solution.py:23
  15.9 0.0 copy-done.2
  15.9 0.0 copy-done.1
  15.9 0.6 fusion.18
  16.5 1.1 add_select_fusion.bits_ref
  17.7 0.3 fusion.21
  17.9 19.1 %steering.1 = (bf16[64,256,512]{2,1,0:T(8,128)(2,1)}, bf16[64,256,512]{2,1,0:T(8,128)(2,1)}) custom-call(s32[1]{0:T(128)} %bitcast.3.base_ref, s32[256,512]{1,0:T(8,128)} %add_select_fusion.bits_ref), custom_call_target="tpu_custom_call" | custom-call | flops 67108864 | bytes 50331648 | tf_op jit(solution)/shard_map/steering/pallas_call | solution.py:280
  37.1 0.7 add_convert_fusion
  37.8 0.0 collective-permute-done
  37.8 0.4 maximum_convert_fusion
  38.2 2.3 %fusion.1 = bf16[8,2,64,1024]{3,2,0,1:T(8,128)(2,1)S(1)} fusion(f32[11,2,64,1024]{3,2,0,1:T(8,128)S(1)} %maximum_convert_fusion, f32[1024]{0:T(1024)S(1)} %bitcast.43, f32[1024]{0:T(1024)S(1)} %bitcast.44, f32[1024]{0:T(1024)S(1)} %bitcast.42, f32[1024]{0:T(1024)S(1)} %bitcast.41), kind=kLoop, calls=%fused_computation.2 | loop fusion | flops 8388608 | bytes 18890752 | tf_op jit(solution)/shard_map/convert_element_type | solution.py:60
  40.5 0.2 fusion.30
  40.7 0.8 fusion.33
  41.5 0.8 fusion.34
  42.3 0.8 fusion.4
  43.1 0.8 fusion.5
  43.9 0.0 copy-start
  43.9 0.1 pad_maximum_fusion
  44.0 30.3 %all_to_all.5 = bf16[8,128,512]{2,1,0:T(8,128)(2,1)} all-to-all(bf16[8,128,512]{2,1,0:T(8,128)(2,1)S(1)} %pad_maximum_fusion), channel_id=1, replica_groups=mesh['group'=2,'chan'=4,'tm'=2,'beam'=2] {'chan','tm'}, dimensions={0} | all-to-all | bytes 2097152 | tf_op jit(solution)/shard_map/all_to_all | solution.py:356
  74.3 0.0 all-gather.3.cloned.1.call-update
  74.3 0.7 broadcast_in_dim.2.flag_ref
  75.0 19.7 %denominators.1.denom_ref = f32[64,1,256]{2,1,0:T(1,128)} custom-call(bf16[64,2,256,512]{3,2,1,0:T(8,128)(2,1)} %model_ref.5, f32[64,2,512]{2,1,0:T(2,128)} %gain_ref.5, s32[64,1,512]{2,1,0:T(1,128)} %broadcast_in_dim.2.flag_ref), custom_call_target="tpu_custom_call" | custom-call | flops 268435456 | bytes 33554432 | tf_op jit(solution)/shard_map/denominators/pallas_call | solution.py:117
  94.8 8.3 %turn.1.x_ref.own_ref = bf16[64,32,512]{2,1,0:T(8,128)(2,1)} custom-call(bf16[2,4,2,128,512]{4,3,2,1,0:T(8,128)(2,1)} %bitcast.29), custom_call_target="tpu_custom_call" | custom-call | bytes 8388608 | tf_op jit(solution)/shard_map/turn/pallas_call | solution.py:187
  103.1 35.7 %correlate.1 = (bf16[64,2,256,512]{3,2,1,0:T(8,128)(2,1)}, f32[64,2,256]{2,1,0:T(2,128)}) custom-call(s32[1]{0:T(128)} %bitcast.beam_ref, bf16[64,32,512]{2,1,0:T(8,128)(2,1)} %turn.1.x_ref.own_ref, bf16[64,32,512]{2,1,0:T(8,128)(2,1)} %turn.1.x_ref.own_ref, bf16[64,2,256,512]{3,2,1,0:T(8,128)(2,1)} %model_ref.5, f32[64,2,512]{2,1,0:T(2,128)} %gain_ref.5, ...), custom_call_target="tpu_custom_call" | custom-call | flops 2147483648 | bytes 67108864 | tf_op jit(solution)/shard_map/correlate/pallas_call | solution.py:212
  138.8 3.6 %all_gather.11.gain_ref = f32[64,2,512]{2,1,0:T(2,128)} all-gather(f32[64,2,256]{2,1,0:T(2,128)} %get-tuple-element.22.older_ref), channel_id=1, replica_groups=mesh['group'=2,'chan'=4,'tm'=2,'beam'=2] {'beam'}, dimensions={2}, use_global_device_ids=true | all-gather | bytes 393216 | tf_op jit(solution)/shard_map/all_gather | solution.py:366
  142.4 23.9 %update.1 = f32[64,2,256]{2,1,0:T(2,128)} custom-call(s32[1]{0:T(128)} %bitcast.beam_ref, bf16[64,32,512]{2,1,0:T(8,128)(2,1)} %turn.1.x_ref.own_ref, bf16[64,32,512]{2,1,0:T(8,128)(2,1)} %turn.1.x_ref.own_ref, bf16[64,2,256,512]{3,2,1,0:T(8,128)(2,1)} %model_ref.5, f32[64,2,512]{2,1,0:T(2,128)} %all_gather.11.gain_ref, ...), custom_call_target="tpu_custom_call" | custom-call | flops 2147483648 | bytes 33554432 | tf_op jit(solution)/shard_map/update/pallas_call | solution.py:212
  166.3 21.6 %beams.1 = f32[64,16,256]{2,1,0:T(8,128)} custom-call(bf16[64,32,512]{2,1,0:T(8,128)(2,1)} %turn.1.x_ref.own_ref, f32[64,2,512]{2,1,0:T(2,128)} %gain_ref.5, s32[64,1,512]{2,1,0:T(1,128)} %broadcast_in_dim.2.flag_ref, bf16[64,256,512]{2,1,0:T(8,128)(2,1)} %get-tuple-element.23.rot_r, bf16[64,256,512]{2,1,0:T(8,128)(2,1)} %get-tuple-element.24.rot_i), custom_call_target="tpu_custom_call" | custom-call | flops 2147483648 | bytes 33554432 | tf_op jit(solution)/shard_map/beams/pallas_call | solution.py:322
  (8 shorter events, 0.1 us)
Async XLA Ops:
  7.2 8.7 %copy-start.2 = (s32[2,256]{1,0:T(2,128)S(1)}, s32[2,256]{1,0:T(2,128)}, u32[]{:S(2)}) copy-start(s32[2,256]{1,0:T(2,128)} %param.10) | copy-start | bytes 6148
  7.2 8.7 %copy-start.1 = (f32[4,1024]{1,0:T(4,128)S(1)}, f32[4,1024]{1,0:T(4,128)}, u32[]{:S(2)}) copy-start(f32[4,1024]{1,0:T(4,128)} %param.7) | copy-start | bytes 49156
  7.2 87.6 %all-gather.3.cloned.1.call-start = ((), (), s32[]{:S(2)}) async-start(), calls=%async_computation.1 | async-start | bytes 3145728 | tf_op jit(solution)/shard_map/all_gather | solution.py:357
  10.9 26.9 %collective-permute-start = (bf16[3,2,64,1024]{3,2,0,1:T(8,128)(2,1)}, bf16[3,2,64,1024]{3,2,0,1:T(8,128)(2,1)S(1)}, u32[]{:S(2)}, u32[]{:S(2)}) collective-permute-start(bf16[3,2,64,1024]{3,2,0,1:T(8,128)(2,1)} %slice.52), channel_id=1, source_target_pairs={{0,2},{1,3},{4,6},{5,7},{8,10},{9,11},{12,14},{13,15},{16,18},{17,... | collective-permute-start | bytes 2359304 | tf_op jit(solution)/shard_map/ppermute | solution.py:23
  43.9 30.4 %copy-start = (s32[64,512]{1,0:T(8,128)S(1)}, s32[64,512]{1,0:T(8,128)}, u32[]{:S(2)}) copy-start(s32[64,512]{1,0:T(8,128)} %param.11) | copy-start | bytes 393220
Sparse Core Ops, SparseCore 0:
  74.4 9.5 all-gather.2
